TPU v7x, 512 devices: a whole 4x4x16 slice. The times are simulated.
512 devices in a mesh: frame: 8 (over y, core), row: 8 (over z_lo), col: 8 (over x, z_hi).
Axes of the slice: x: 4, y: 4, z: 16 (z_hi: 2, z_lo: 8; z = z_hi * 8 + z_lo), core: 2. Of those that a mesh axis runs over, the one named last changes fastest.
Arguments:
- frames_in: bfloat16 [32, 64, 64, 1024], P('frame', 'row', None, 'col'), may hold values from -6 to 6
- spatial_weight: bfloat16 [9, 1024, 1024], P(None, ('frame', 'row'), 'col'), may hold values from -0.0625 to 0.0625
- temporal_weight: bfloat16 [3, 1024, 1024], P(None, ('frame', 'row'), 'col'), may hold values from -0.109375 to 0.109375
- spatial_bias: float32 [1024], P('col'), may hold values from -3 to 3
- temporal_bias: float32 [1024], P('col'), may hold values from -3 to 3
- clip_id: int32 [32], replicated, may hold values from 0 to 7, as said below
Outputs:
- block_out: bfloat16 [32, 64, 64, 1024], P('frame', 'row', None, 'col')
Inputs may be any that keep to these rules, and one draw needn't show every extreme that they name: `clip_id`: clip numbers of the frames in order, never falling; each clip has 1 to 7 frames and one has exactly 7.
All inputs are finite; a program needn't handle non-finite values.
Results may differ from a plain program's by a relative error of at most 0.01.
Values may be sent and summed in bfloat16 or wider, within the bound.
A program may use at most 64 MiB of HBM per device.

v0:
```python
import jax
import jax.numpy as jnp
from jax import lax
from jax.sharding import PartitionSpec as P


def with_halo(block, sides, width):
    for axis, dim in sides:
        count = lax.axis_size(axis)
        forward = [(i, i + 1) for i in range(count - 1)]
        backward = [(target, source) for source, target in forward]
        low = lax.ppermute(
            lax.slice_in_dim(block, block.shape[dim] - width, None, axis=dim), axis, forward
        )
        high = lax.ppermute(lax.slice_in_dim(block, 0, width, axis=dim), axis, backward)
        block = jnp.concatenate([low, block, high], axis=dim)
    return block


def spatial_terms(total, gathered, weights):
    row_count = total.shape[1]
    wide = total.shape[2]
    for tap in range(9):
        shift_y, shift_x = (tap // 3, tap % 3)
        window = gathered[:, shift_y : shift_y + row_count, shift_x : shift_x + wide, :]
        total = total + jnp.einsum(
            "fhwc,cd->fhwd", window, weights[tap], preferred_element_type=jnp.float32
        )
    return total


def temporal_terms(sources, weights):
    result = []
    for tap in range(3):
        window = sources[tap]
        result.append(
            jnp.einsum("fhwc,cd->fhwd", window, weights[tap], preferred_element_type=jnp.float32)
        )
    return (result[0], result[1], result[2])


def body(frames_in, spatial_weight, temporal_weight, spatial_bias, temporal_bias, clip_id):
    fr_count, row_count, wide, col_width = frames_in.shape
    rimmed = with_halo(frames_in, (("row", 1),), 1)
    gathered = lax.all_gather(rimmed, "col", axis=3, tiled=True)
    gathered = jnp.pad(gathered, ((0, 0), (0, 0), (1, 1), (0, 0)))
    blank = jnp.zeros((fr_count, row_count, wide, col_width), jnp.float32)
    full_spatial, full_temporal = (
        lax.all_gather(spatial_weight, ("frame", "row"), axis=1, tiled=True),
        lax.all_gather(temporal_weight, ("frame", "row"), axis=1, tiled=True),
    )
    spatial = spatial_terms(blank, gathered, full_spatial)
    hidden = (spatial + spatial_bias).astype(jnp.bfloat16)
    active = jax.nn.silu(hidden.astype(jnp.float32)).astype(jnp.bfloat16)
    index = lax.axis_index("frame")
    edge_ids = jnp.full((1,), -1, jnp.int32)
    padded_ids = jnp.concatenate([edge_ids, clip_id, edge_ids])
    local_ids = lax.dynamic_slice_in_dim(padded_ids, index * fr_count, fr_count + 2)
    prev_ok = (local_ids[1:-1] == local_ids[:-2]).astype(jnp.float32).reshape(fr_count, 1, 1, 1)
    next_ok = (local_ids[1:-1] == local_ids[2:]).astype(jnp.float32).reshape(fr_count, 1, 1, 1)
    source = with_halo(active, (("frame", 0),), 1)
    whole = lax.all_gather(source, "col", axis=3, tiled=True)
    sources = (whole[:-2], whole[1:-1], whole[2:])
    taps = temporal_terms(sources, full_temporal)
    before, after = (taps[0], taps[2])
    total = (
        hidden.astype(jnp.float32) + temporal_bias + prev_ok * before + taps[1] + next_ok * after
    )
    return total.astype(jnp.bfloat16)


def solution(mesh):
    placed = (
        P("frame", "row", None, "col"),
        P(None, ("frame", "row"), "col"),
        P(None, ("frame", "row"), "col"),
        P("col"),
        P("col"),
        P(),
    )
    return jax.shard_map(
        body, mesh=mesh, in_specs=placed, out_specs=P("frame", "row", None, "col"), check_vma=False
    )
```

profile of v0, /device:TPU:266, one launch (start us, length us, event | category | flops | bytes accessed | tf_op | source)
XLA Modules:
  0.0 734.2 jit_solution(9733512047469235792)
XLA Ops:
  6.5 0.7 all-gather.6.cloned.1.call-update
  7.3 0.9 fusion.65
  8.2 2.9 collective-permute-start
  11.1 1.3 collective-permute-start.1
  12.4 0.6 collective-permute-done
  13.0 4.3 collective-permute-done.1
  17.3 2.0 pad_maximum_fusion.1
  19.3 0.0 all-gather.8.cloned.1.call-start
  19.4 142.3 %all-gather.6.cloned.1.call-done = bf16[9,1024,128]{2,1,0:T(8,128)(2,1)} async-done(((bf16[9,16,128]{2,1,0:T(8,128)(2,1)}), bf16[9,1024,128]{2,1,0:T(8,128)(2,1)}) %all-gather.6.cloned.1.call-update) | async-done | bytes 2359312 | tf_op jit(solution)/shard_map/all_gather | solution.py:49
  161.7 175.7 %all-gather.4.cloned.1.call-done = bf16[4,10,64,1024]{3,2,1,0:T(8,128)(2,1)} async-done(((bf16[4,10,64,128]{3,2,1,0:T(8,128)(2,1)}), bf16[4,10,64,1024]{3,2,1,0:T(8,128)(2,1)}) %all-gather.4.cloned.1.call-update) | async-done | bytes 5242896 | tf_op jit(solution)/shard_map/all_gather | solution.py:45
  337.4 3.6 fusion
  341.1 0.2 copy-done
  341.3 2.2 fusion.2
  343.5 1.3 fusion.4
  344.8 1.3 fusion.55
  346.1 1.3 fusion.56
  347.3 1.3 fusion.57
  348.6 1.3 fusion.6
  349.9 1.3 fusion.8
  351.2 1.9 fusion.54
  353.2 1.9 collective-permute-start.2
  355.1 3.6 collective-permute-start.3
  358.7 0.7 collective-permute-done.2
  359.5 1.8 collective-permute-done.3
  361.2 1.0 pad_maximum_fusion
  362.3 0.1 pad_add_fusion
  362.3 0.1 dynamic_slice.3
  362.4 0.1 compare_convert_fusion.1
  362.5 355.9 %all_gather.15 = bf16[3,1024,128]{2,1,0:T(8,128)(2,1)S(1)} all-gather(bf16[3,16,128]{2,1,0:T(8,128)(2,1)S(1)} %copy-done.3), channel_id=1, replica_groups=mesh['frame'=8,'row'=8,'col'=8] {'frame','row'}, dimensions={1}, use_global_device_ids=true | all-gather | bytes 798720 | tf_op jit(solution)/shard_map/all_gather | solution.py:50
  718.4 3.6 convolution_multiply_fusion
  722.0 3.4 fusion.19
  725.5 2.1 fusion.50
  (19 shorter events, 0.1 us)
Async XLA Ops:
  6.5 155.2 %all-gather.6.cloned.1.call-start = ((), (), s32[]{:S(2)}) async-start(), calls=%async_computation.1 | async-start | bytes 2396160 | tf_op jit(solution)/shard_map/all_gather | solution.py:49
  7.3 330.2 %all-gather.4.cloned.1.call-start = ((), (), s32[]{:S(2)}) async-start(), calls=%async_computation | async-start | bytes 5898240 | tf_op jit(solution)/shard_map/all_gather | solution.py:45
  8.2 4.8 collective-permute-start
  11.1 6.2 collective-permute-start.1
  19.3 699.1 %all-gather.8.cloned.1.call-start = ((), (), s32[]{:S(2)}) async-start(), calls=%async_computation.2 | async-start | bytes 7077888 | tf_op jit(solution)/shard_map/all_gather | solution.py:62
  337.4 3.8 copy-start
  337.4 6.1 copy-start.2
  348.6 2.6 copy-start.5
  351.1 11.1 %copy-start.6 = (s32[32]{0:T(128)S(1)}, s32[32]{0:T(128)}, u32[]{:S(2)}) copy-start(s32[32]{0:T(128)} %param.11) | copy-start | bytes 388
  351.2 11.3 %copy-start.3 = (bf16[3,16,128]{2,1,0:T(8,128)(2,1)S(1)}, bf16[3,16,128]{2,1,0:T(8,128)(2,1)}, u32[]{:S(2)}) copy-start(bf16[3,16,128]{2,1,0:T(8,128)(2,1)} %param.8) | copy-start | bytes 36868
  353.1 368.9 %copy-start.4 = (f32[128]{0:T(128)S(1)}, f32[128]{0:T(128)}, u32[]{:S(2)}) copy-start(f32[128]{0:T(128)} %param.10) | copy-start | bytes 1540
  353.2 6.3 collective-permute-start.2
  355.1 6.1 collective-permute-start.3
  718.4 7.1 copy-start.1
Sparse Core Ops, SparseCore 0:
  9.4 152.2 all-gather.5
  164.8 172.6 all-gather.3
  362.4 233.3 all-gather.7
where the time goes:
time: 734 us
  blocking collectives  356 us (49%)
  waiting for transfers between devices  326 us (44%)
  matrix products  24.6 us (3%)
  between operations  13.3 us (2%)
  starting transfers between devices  9.86 us (1%)
    all_gather x1, blocking collectives, body(): lax.all_gather(temporal_weight, ('frame', 'row'), axis=1, tiled=True)  356 us
    all_gather x1, waiting for transfers between devices, body(): gathered = lax.all_gather(rimmed, 'col', axis=3, tiled=True)  176 us
    all_gather x1, waiting for transfers between devices, body(): lax.all_gather(spatial_weight, ('frame', 'row'), axis=1, tiled=True)  142 us
    dot_general x9, matrix products, spatial_terms(): jnp.einsum('fhwc,cd->fhwd', window, weights[tap], preferred_element_type=...  15.4 us
  transfers between devices with their start and end apart: 7, of which 6 were waited for; matrix products, arithmetic and copies ran while one was open for 0% of the time, Pallas kernels for 0%

commit v1 on v0

--- a/solution.py
+++ b/solution.py
@@ -42,7 +42,9 @@
 def body(frames_in, spatial_weight, temporal_weight, spatial_bias, temporal_bias, clip_id):
     fr_count, row_count, wide, col_width = frames_in.shape
     rimmed = with_halo(frames_in, (("row", 1),), 1)
-    gathered = lax.all_gather(rimmed, "col", axis=3, tiled=True)
+    gathered = jnp.concatenate(
+        lax.all_to_all(jnp.stack([rimmed] * lax.axis_size("col")), "col", 0, 0), axis=3
+    )
     gathered = jnp.pad(gathered, ((0, 0), (0, 0), (1, 1), (0, 0)))
     blank = jnp.zeros((fr_count, row_count, wide, col_width), jnp.float32)
     full_spatial, full_temporal = (

time: 734 us -> 754 us (1.027)
  the two profiles are of different devices: /device:TPU:266 before, /device:TPU:4 now
where the time goes in v1:
time: 754 us; the launch traced here: 753 us
  waiting for transfers between devices  354 us (47%)
  blocking collectives  315 us (42%)
  matrix products  30.6 us (4%)
  starting transfers between devices  26 us (3%)
  between operations  13.6 us (2%)
  local copies, waits for them, and re-layouts  10.7 us (1%)
    all_gather x1, blocking collectives, body(): lax.all_gather(temporal_weight, ('frame', 'row'), axis=1, tiled=True)  315 us
    all_gather x1, waiting for transfers between devices, body(): lax.all_gather(spatial_weight, ('frame', 'row'), axis=1, tiled=True)  236 us
    all_to_all x1, waiting for transfers between devices, body(): lax.all_to_all(jnp.stack([rimmed] * lax.axis_size('col')), 'col', 0, 0)  109 us
    dot_general x9, matrix products, spatial_terms(): jnp.einsum('fhwc,cd->fhwd', window, weights[tap], preferred_element_type=...  21.4 us
    all_to_all x1, starting transfers between devices, body(): lax.all_to_all(jnp.stack([rimmed] * lax.axis_size('col')), 'col', 0, 0)  17.2 us
  transfers between devices with their start and end apart: 7, of which 5 were waited for; matrix products, arithmetic and copies ran while one was open for 1% of the time, Pallas kernels for 0%

profile of v1, /device:TPU:4, one launch (start us, length us, event | category | flops | bytes accessed | tf_op | source)
XLA Modules:
  0.0 753.1 jit_solution(620829263147515091)
XLA Ops:
  6.5 0.9 fusion.39
  7.4 3.8 collective-permute-start
  11.3 1.3 collective-permute-start.1
  12.6 0.6 collective-permute-done
  13.1 4.3 collective-permute-done.1
  17.4 1.1 pad_maximum_fusion.1
  18.5 3.7 stack.2
  22.2 17.2 %all-to-all-start = ((bf16[8,4,10,64,128]{4,3,2,1,0:T(8,128)(2,1)}), bf16[8,4,10,64,128]{4,3,2,1,0:T(8,128)(2,1)}, u32[]{:S(2)}, u32[]{:S(2)}) async-start(bf16[8,4,10,64,128]{4,3,2,1,0:T(8,128)(2,1)} %stack.2), calls=%async_computation | async-start | bytes 10485760 | tf_op jit(solution)/shard_map/all_to_all | solution.py:46
  39.4 0.7 all-gather.3.cloned.1.call-update
  40.2 109.4 %all-to-all-done = bf16[8,4,10,64,128]{4,3,2,1,0:T(8,128)(2,1)} async-done(((bf16[8,4,10,64,128]{4,3,2,1,0:T(8,128)(2,1)}), bf16[8,4,10,64,128]{4,3,2,1,0:T(8,128)(2,1)}, u32[]{:S(2)}, u32[]{:S(2)}) %all-to-all-start) | async-done | bytes 5242912 | tf_op jit(solution)/shard_map/all_to_all | solution.py:46
  149.6 5.8 copy_bitcast_fusion
  155.4 235.9 %all-gather.3.cloned.1.call-done = bf16[9,1024,128]{2,1,0:T(8,128)(2,1)} async-done(((bf16[9,16,128]{2,1,0:T(8,128)(2,1)}), bf16[9,1024,128]{2,1,0:T(8,128)(2,1)}) %all-gather.3.cloned.1.call-update) | async-done | bytes 2359312 | tf_op jit(solution)/shard_map/all_gather | solution.py:51
  391.3 3.6 fusion.10
  395.0 0.2 copy-done.1
  395.1 2.2 fusion.6
  397.4 1.3 fusion.8
  398.7 1.3 fusion.2
  399.9 1.3 fusion.4
  401.2 1.3 fusion
  402.5 3.5 fusion.25
  406.0 3.5 fusion.23
  409.6 3.5 fusion.31
  413.1 2.2 collective-permute-start.2
  415.3 1.5 collective-permute-start.3
  416.8 3.5 collective-permute-done.3
  420.3 1.0 pad_maximum_fusion
  421.4 0.1 pad_add_fusion
  421.4 0.1 dynamic_slice.3
  421.6 315.4 %all_gather.11 = bf16[3,1024,128]{2,1,0:T(8,128)(2,1)S(1)} all-gather(bf16[3,16,128]{2,1,0:T(8,128)(2,1)S(1)} %copy-done.3), channel_id=1, replica_groups=mesh['frame'=8,'row'=8,'col'=8] {'frame','row'}, dimensions={1}, use_global_device_ids=true | all-gather | bytes 798720 | tf_op jit(solution)/shard_map/all_gather | solution.py:52
  737.1 3.6 convolution_multiply_fusion
  740.7 3.5 fusion.19
  744.2 2.1 fusion.26
  (20 shorter events, 0.2 us)
Async XLA Ops:
  7.4 5.7 collective-permute-start
  11.3 6.2 collective-permute-start.1
  22.2 127.3 %all-to-all-start = ((bf16[8,4,10,64,128]{4,3,2,1,0:T(8,128)(2,1)}), bf16[8,4,10,64,128]{4,3,2,1,0:T(8,128)(2,1)}, u32[]{:S(2)}, u32[]{:S(2)}) async-start(bf16[8,4,10,64,128]{4,3,2,1,0:T(8,128)(2,1)} %stack.2), calls=%async_computation | async-start | bytes 10485760 | tf_op jit(solution)/shard_map/all_to_all | solution.py:46
  39.4 351.9 %all-gather.3.cloned.1.call-start = ((), (), s32[]{:S(2)}) async-start(), calls=%async_computation.1 | async-start | bytes 2396160 | tf_op jit(solution)/shard_map/all_gather | solution.py:51
  40.1 696.9 %all-gather.5.cloned.1.call-start = ((), (), s32[]{:S(2)}) async-start(), calls=%async_computation.2 | async-start | bytes 7077888 | tf_op jit(solution)/shard_map/all_gather | solution.py:64
  391.3 3.8 copy-start.1
  391.3 6.1 copy-start.2
  406.0 3.5 copy-start.5
  409.5 11.8 %copy-start.6 = (s32[32]{0:T(128)S(1)}, s32[32]{0:T(128)}, u32[]{:S(2)}) copy-start(s32[32]{0:T(128)} %param.11) | copy-start | bytes 388
  409.5 12.1 %copy-start.3 = (bf16[3,16,128]{2,1,0:T(8,128)(2,1)S(1)}, bf16[3,16,128]{2,1,0:T(8,128)(2,1)}, u32[]{:S(2)}) copy-start(bf16[3,16,128]{2,1,0:T(8,128)(2,1)} %param.8) | copy-start | bytes 36868
  413.1 327.6 %copy-start.4 = (f32[128]{0:T(128)S(1)}, f32[128]{0:T(128)}, u32[]{:S(2)}) copy-start(f32[128]{0:T(128)} %param.10) | copy-start | bytes 1540
  413.1 3.7 collective-permute-start.2
  415.3 5.0 collective-permute-start.3
  737.0 7.1 copy-start
Sparse Core Ops, SparseCore 0:
  42.2 349.0 all-gather.2
  421.5 249.7 all-gather.4
